TPU v7x, 32 devices: a whole 2x2x4 slice. The times are simulated.
32 devices in a mesh: dp: 4 (over y, x), vocab: 8 (over z, core).
Axes of the slice: x: 2, y: 2, z: 4, core: 2. Of those that a mesh axis runs over, the one named last changes fastest.
Arguments:
- hidden: bfloat16 [1024, 5120], P('dp')
- head_t: bfloat16 [5120, 19456], P('dp', 'vocab'), may hold values from -0.25 to 0.25
- targets: int32 [1024], P('dp'), may hold values from 0 to 19455
- token_ids: int32 [1024], P('dp'), may hold values from 0 to 19455, as said below
- embed_cot: bfloat16 [1024, 5120], P('dp'), may hold values from -6 to 6
Outputs:
- head_grad: bfloat16 [5120, 19456], P('dp', 'vocab')
- embed_grad: bfloat16 [5120, 19456], P('dp', 'vocab')
- hidden_grad: bfloat16 [1024, 5120], P('vocab', 'dp')
Inputs may be any that keep to these rules, and one draw needn't show every extreme that they name: `token_ids`: among the 256 input ids of one data group, at most 64 lie in any one block of 2432 vocabulary rows that starts at a multiple of 2432; in every group some block holds exactly 64.
All inputs are finite; a program needn't handle non-finite values.
Results may differ from a plain program's by a relative error of at most 0.0033.
Values may be sent and summed in bfloat16 or wider, within the bound.
A program may use at most 128 MiB of HBM per device.

v0:
```python
import jax
import jax.numpy as jnp
from jax import lax
from jax.sharding import PartitionSpec as P


def on_device(hidden, head_t, targets, token_ids, embed_cot):
    width_dev = head_t.shape[1]
    offset = lax.axis_index("vocab") * width_dev
    all_ids = lax.all_gather(token_ids, "dp", axis=0, tiled=True)
    columns = offset + jnp.arange(width_dev, dtype=jnp.int32)[None, :]
    local_hidden, local_cot = (
        lax.all_to_all(hidden, "dp", split_axis=1, concat_axis=0, tiled=True),
        lax.all_to_all(embed_cot, "dp", split_axis=1, concat_axis=0, tiled=True),
    )
    id_hot = (columns == all_ids[:, None]).astype(jnp.bfloat16)
    embed_grad = lax.dot_general(
        local_cot, id_hot, (((0,), (0,)), ((), ())), preferred_element_type=jnp.float32
    ).astype(jnp.bfloat16)
    logits = lax.psum_scatter(
        jnp.dot(local_hidden, head_t, preferred_element_type=jnp.float32),
        "dp",
        scatter_dimension=0,
        tiled=True,
    )
    row_max = lax.pmax(jnp.max(logits, axis=1, keepdims=True), "vocab")
    expo = jnp.exp(logits - row_max)
    row_sum = lax.psum(jnp.sum(expo, axis=1, keepdims=True), "vocab")
    target_hot = (columns == targets[:, None]).astype(jnp.float32)
    dlogits = (expo / row_sum - target_hot).astype(jnp.bfloat16)
    all_grads = lax.all_gather(dlogits, "dp", axis=0, tiled=True)
    head_grad = lax.dot_general(
        local_hidden, all_grads, (((0,), (0,)), ((), ())), preferred_element_type=jnp.float32
    ).astype(jnp.bfloat16)
    hidden_grad = lax.psum_scatter(
        lax.dot_general(
            all_grads, head_t, (((1,), (1,)), ((), ())), preferred_element_type=jnp.float32
        ),
        "vocab",
        scatter_dimension=0,
        tiled=True,
    ).astype(jnp.bfloat16)
    return (head_grad, embed_grad, hidden_grad)


def solution(mesh):
    placed = (P("dp", None), P("dp", "vocab"), P("dp"), P("dp"), P("dp", None))
    return jax.shard_map(
        on_device,
        mesh=mesh,
        in_specs=placed,
        out_specs=(P("dp", "vocab"), P("dp", "vocab"), P("vocab", "dp")),
        check_vma=False,
    )
```

profile of v0, /device:TPU:0, one launch (start us, length us, event | category | flops | bytes accessed | tf_op | source)
XLA Modules:
  0.0 358.3 jit_solution(14743323993973278830)
XLA Ops:
  7.2 0.0 reduce-scatter.3.cloned.1.call-start
  7.2 4.4 %copy.18 = bf16[256,5120]{0,1:T(8,128)(2,1)} copy(bf16[256,5120]{1,0:T(8,128)(2,1)} %param.5) | data formatting | bytes 5242880 | tf_op args[0]
  11.6 36.2 %all_to_all.38 = bf16[256,4,1280]{0,2,1:T(8,128)(2,1)S(1)} all-to-all(bf16[256,4,1280]{0,2,1:T(8,128)(2,1)} %bitcast.22), channel_id=1, replica_groups=mesh['dp'=4,'vocab'=8] {'dp'}, dimensions={1} | all-to-all | bytes 5242880 | tf_op jit(solution)/shard_map/all_to_all | solution.py:13
  47.8 2.6 copy.19
  50.4 12.5 %fusion.8 = f32[1024,2432]{1,0:T(8,128)} fusion(bf16[1024,1280]{1,0:T(8,128)(2,1)} %bitcast.23, bf16[1280,2432]{1,0:T(8,128)(2,1)} %param.6), kind=kOutput, calls=%fused_computation.11 | convolution fusion | flops 6375342080 | bytes 18808832 | tf_op jit(solution)/shard_map/dot_general | solution.py:21
  62.9 0.0 reduce-scatter.3.cloned.1.call-update
  62.9 0.0 copy-start.3
  62.9 0.0 all-gather.3.cloned.1.call-start
  63.0 99.1 %reduce-scatter.3.cloned.1.call-done = f32[256,2432]{1,0:T(8,128)} async-done(((f32[1024,2432]{1,0:T(8,128)}), f32[256,2432]{1,0:T(8,128)}) %reduce-scatter.3.cloned.1.call-update) | async-done | bytes 2490384 | tf_op jit(solution)/shard_map/reduce_scatter | solution.py:20
  162.1 0.0 copy-start
  162.1 2.1 reduce_max.9
  164.2 16.2 %pmax.7 = f32[256]{0:T(256)S(1)} all-reduce(f32[256]{0:T(256)S(1)} %reduce_max.9), channel_id=1, replica_groups=mesh['dp'=4,'vocab'=8] {'vocab'}, use_global_device_ids=true, to_apply=%region_2.0 | all-reduce | flops 256 | bytes 2048 | tf_op jit(solution)/shard_map/pmax | solution.py:26
  180.4 0.0 copy-done
  180.4 0.5 fusion.7
  180.9 13.6 %psum.7 = f32[256]{0:T(256)S(1)} all-reduce(f32[256]{0:T(256)S(1)} %fusion.7), channel_id=1, replica_groups=mesh['dp'=4,'vocab'=8] {'vocab'}, use_global_device_ids=true, to_apply=%region_4.0 | all-reduce | flops 256 | bytes 2048 | tf_op jit(solution)/shard_map/psum | solution.py:28
  194.5 0.0 copy-done.3
  194.5 1.8 subtract_convert_fusion
  196.2 0.0 all-gather.3.cloned.1.call-update
  196.3 0.0 reduce-scatter.5.cloned.1.call-start
  196.3 56.5 %all-gather.3.cloned.1.call-done = bf16[1024,2432]{1,0:T(8,128)(2,1)} async-done(((bf16[256,2432]{1,0:T(8,128)(2,1)}), bf16[1024,2432]{1,0:T(8,128)(2,1)}) %all-gather.3.cloned.1.call-update) | async-done | bytes 4980752 | tf_op jit(solution)/shard_map/all_gather | solution.py:31
  252.8 12.3 %fusion.9 = f32[1024,1280]{1,0:T(8,128)} fusion(bf16[1024,2432]{1,0:T(8,128)(2,1)} %all-gather.3.cloned.1.call-done, bf16[1280,2432]{1,0:T(8,128)(2,1)} %param.6), kind=kOutput, calls=%fused_computation.12 | convolution fusion | flops 6375342080 | bytes 16449536 | tf_op jit(solution)/shard_map/dot_general | solution.py:36
  265.0 0.0 copy-start.1
  265.0 0.0 reduce-scatter.5.cloned.1.call-update
  265.0 1.7 copy-done.1
  266.8 2.5 copy.20
  269.3 0.0 copy-start.4
  269.3 3.8 %all-to-all-start.1 = ((bf16[256,4,1280]{0,2,1:T(8,128)(2,1)}), bf16[256,4,1280]{0,2,1:T(8,128)(2,1)S(1)}, u32[]{:S(2)}, u32[]{:S(2)}) async-start(bf16[256,4,1280]{0,2,1:T(8,128)(2,1)} %bitcast.20), calls=%async_computation.2 | async-start | bytes 5242880 | tf_op jit(solution)/shard_map/all_to_all | solution.py:14
  273.1 0.0 copy-done.4
  273.1 32.2 %all-gather = s32[4,1,256]{2,1,0:T(1,128)S(1)} all-gather(s32[1,1,256]{2,1,0:T(1,128)S(1)} %bitcast.27), channel_id=1, replica_groups=mesh['dp'=4,'vocab'=8] {'dp'}, dimensions={0}, use_global_device_ids=true | all-gather | bytes 5120 | tf_op jit(solution)/shard_map/all_gather | solution.py:10
  305.3 0.0 all-to-all-done.1
  305.3 2.6 copy.21
  307.9 10.9 %fusion.2 = bf16[1280,2432]{0,1:T(8,128)(2,1)} fusion(bf16[1024,1280]{1,0:T(8,128)(2,1)} %bitcast.25, s32[2432]{0:T(1024)S(1)} %iota_add_fusion, s32[1024]{0:T(1024)S(1)} %bitcast.26), kind=kOutput, calls=%fused_computation.4 | convolution fusion | flops 6380945408 | bytes 8861184 | tf_op jit(solution)/shard_map/dot_general | solution.py:17
  318.7 0.0 copy-start.2
  318.7 9.5 %copy.23 = bf16[1280,2432]{1,0:T(8,128)(2,1)} copy(bf16[1280,2432]{0,1:T(8,128)(2,1)} %fusion.2) | data formatting | bytes 12451840
  328.2 0.0 copy-done.2
  328.2 12.3 %fusion.1 = bf16[1280,2432]{0,1:T(8,128)(2,1)} fusion(bf16[1024,2432]{1,0:T(8,128)(2,1)} %all-gather.3.cloned.1.call-done, bf16[1024,1280]{1,0:T(8,128)(2,1)S(1)} %bitcast.24), kind=kOutput, calls=%fused_computation.3 | convolution fusion | flops 6378455040 | bytes 13828096 | tf_op jit(solution)/shard_map/dot_general | solution.py:32
  340.6 9.3 %copy.22 = bf16[1280,2432]{1,0:T(8,128)(2,1)} copy(bf16[1280,2432]{0,1:T(8,128)(2,1)} %fusion.1) | data formatting | bytes 12451840
  349.9 0.0 reduce-scatter.5.cloned.1.call-done
  349.9 1.8 convert_element_type.28
  (1 shorter events, 0.0 us)
Async XLA Ops:
  7.2 155.0 %reduce-scatter.3.cloned.1.call-start = ((), (), s32[]{:S(2)}) async-start(), calls=%async_computation.4 | async-start | bytes 12451840 | tf_op jit(solution)/shard_map/reduce_scatter | solution.py:20
  62.9 131.6 %copy-start.3 = (s32[256]{0:T(256)S(1)}, s32[256]{0:T(256)}, u32[]{:S(2)}) copy-start(s32[256]{0:T(256)} %param.7) | copy-start | bytes 3076
  62.9 189.8 %all-gather.3.cloned.1.call-start = ((), (), s32[]{:S(2)}) async-start(), calls=%async_computation.5 | async-start | bytes 6225920 | tf_op jit(solution)/shard_map/all_gather | solution.py:31
  162.1 18.3 %copy-start = (f32[256,2432]{1,0:T(8,128)S(1)}, f32[256,2432]{1,0:T(8,128)}, u32[]{:S(2)}) copy-start(f32[256,2432]{1,0:T(8,128)} %reduce-scatter.3.cloned.1.call-done) | copy-start | bytes 7471108
  196.3 153.6 %reduce-scatter.5.cloned.1.call-start = ((), (), s32[]{:S(2)}) async-start(), calls=%async_computation.6 | async-start | bytes 5898240 | tf_op jit(solution)/shard_map/reduce_scatter | solution.py:35
  265.0 1.7 copy-start.1
  269.3 3.8 %copy-start.4 = (s32[256]{0:T(256)S(1)}, s32[256]{0:T(256)}, u32[]{:S(2)}) copy-start(s32[256]{0:T(256)} %param.8) | copy-start | bytes 3076
  269.3 36.0 %all-to-all-start.1 = ((bf16[256,4,1280]{0,2,1:T(8,128)(2,1)}), bf16[256,4,1280]{0,2,1:T(8,128)(2,1)S(1)}, u32[]{:S(2)}, u32[]{:S(2)}) async-start(bf16[256,4,1280]{0,2,1:T(8,128)(2,1)} %bitcast.20), calls=%async_computation.2 | async-start | bytes 5242880 | tf_op jit(solution)/shard_map/all_to_all | solution.py:14
  318.7 9.5 %copy-start.2 = (bf16[4,256,1280]{2,1,0:T(8,128)(2,1)S(1)}, bf16[4,256,1280]{2,1,0:T(8,128)(2,1)}, u32[]{:S(2)}) copy-start(bf16[4,256,1280]{2,1,0:T(8,128)(2,1)} %copy.19) | copy-start | bytes 7864324
Sparse Core Ops, SparseCore 0:
  63.0 99.0 reduce-scatter.2
  196.4 56.3 all-gather.2
  265.2 59.8 reduce-scatter.4
where the time goes:
time: 359 us; the launch traced here: 358 us
  waiting for transfers between devices  156 us (43%)
  blocking collectives  98.2 us (27%)
  matrix products  48 us (13%)
  local copies, waits for them, and re-layouts  32.6 us (9%)
  between operations  13.8 us (4%)
  other arithmetic  6.14 us (2%)
  starting transfers between devices  3.93 us (1%)
    reduce_scatter x1, waiting for transfers between devices, on_device(): lax.psum_scatter(jnp.dot(local_hidden, head_t, preferred_element_type=jnp...  99.1 us
    all_gather x1, waiting for transfers between devices, on_device(): all_grads = lax.all_gather(dlogits, 'dp', axis=0, tiled=True)  56.5 us
    all_to_all x1, blocking collectives, on_device(): lax.all_to_all(hidden, 'dp', split_axis=1, concat_axis=0, tiled=True)  36.2 us
    all_gather x1, blocking collectives, on_device(): all_ids = lax.all_gather(token_ids, 'dp', axis=0, tiled=True)  32.2 us
    unnamed x14, local copies, waits for them, and re-layouts  27.5 us
    pmax x1, blocking collectives, on_device(): row_max = lax.pmax(jnp.max(logits, axis=1, keepdims=True), 'vocab')  16.2 us
    psum x1, blocking collectives, on_device(): row_sum = lax.psum(jnp.sum(expo, axis=1, keepdims=True), 'vocab')  13.6 us
    dot_general x1, matrix products, on_device(): jnp.dot(local_hidden, head_t, preferred_element_type=jnp.float32)  12.5 us
  transfers between devices with their start and end apart: 4, of which 2 were waited for; matrix products, arithmetic and copies ran while one was open for 13% of the time, Pallas kernels for 0%

commit v1 on v0

--- a/solution.py
+++ b/solution.py
@@ -2,6 +2,13 @@
 import jax.numpy as jnp
 from jax import lax
 from jax.sharding import PartitionSpec as P
+
+
+def trade_parts(x, name, split, join):
+    peers = lax.axis_size(name)
+    blocks = jnp.stack(jnp.split(x, peers, axis=split), axis=0)
+    blocks = lax.all_to_all(blocks, name, split_axis=0, concat_axis=0)
+    return jnp.concatenate(blocks, axis=join)
 
 
 def on_device(hidden, head_t, targets, token_ids, embed_cot):
@@ -10,7 +17,7 @@
     all_ids = lax.all_gather(token_ids, "dp", axis=0, tiled=True)
     columns = offset + jnp.arange(width_dev, dtype=jnp.int32)[None, :]
     local_hidden, local_cot = (
-        lax.all_to_all(hidden, "dp", split_axis=1, concat_axis=0, tiled=True),
+        trade_parts(hidden, "dp", 1, 0),
         lax.all_to_all(embed_cot, "dp", split_axis=1, concat_axis=0, tiled=True),
     )
     id_hot = (columns == all_ids[:, None]).astype(jnp.bfloat16)

time: 359 us -> 342 us (0.953)
  local copies, waits for them, and re-layouts: 32.6 us -> 19.9 us
  matrix products: 48 us -> 43.6 us
    unnamed x14 -> x18, local copies, waits for them, and re-layouts: 27.5 us -> 15.3 us
  transfers between devices with their start and end apart: 4 -> 4, of which waited for: 2 -> 2; matrix products, arithmetic and copies ran while one was open for 13% -> 11% of each run, Pallas kernels for 0% -> 0%
where the time goes in v1:
time: 342 us; the launch traced here: 341 us
  waiting for transfers between devices  155 us (45%)
  blocking collectives  98.1 us (29%)
  matrix products  43.6 us (13%)
  local copies, waits for them, and re-layouts  19.9 us (6%)
  between operations  13.8 us (4%)
  other arithmetic  6.47 us (2%)
  starting transfers between devices  3.93 us (1%)
    reduce_scatter x1, waiting for transfers between devices, on_device(): lax.psum_scatter(jnp.dot(local_hidden, head_t, preferred_element_type=jnp...  99 us
    all_gather x1, waiting for transfers between devices, on_device(): all_grads = lax.all_gather(dlogits, 'dp', axis=0, tiled=True)  56.5 us
    all_to_all x1, blocking collectives, trade_parts(): blocks = lax.all_to_all(blocks, name, split_axis=0, concat_axis=0)  36.1 us
    all_gather x1, blocking collectives, on_device(): all_ids = lax.all_gather(token_ids, 'dp', axis=0, tiled=True)  32.2 us
    pmax x1, blocking collectives, on_device(): row_max = lax.pmax(jnp.max(logits, axis=1, keepdims=True), 'vocab')  16.2 us
    unnamed x18, local copies, waits for them, and re-layouts  15.3 us
    psum x1, blocking collectives, on_device(): row_sum = lax.psum(jnp.sum(expo, axis=1, keepdims=True), 'vocab')  13.6 us
    dot_general x1, matrix products, on_device(): lax.dot_general(all_grads, head_t, (((1,), (1,)), ((), ())), preferred_el...  12.2 us
  transfers between devices with their start and end apart: 4, of which 2 were waited for; matrix products, arithmetic and copies ran while one was open for 11% of the time, Pallas kernels for 0%

profile of v1, /device:TPU:0, one launch (start us, length us, event | category | flops | bytes accessed | tf_op | source)
XLA Modules:
  0.0 341.3 jit_solution(13375268797704114774)
XLA Ops:
  7.2 0.0 reduce-scatter.3.cloned.1.call-start
  7.2 0.0 slice-start
  7.2 2.0 slice_bitcast_fusion.3
  9.2 0.0 slice-start.1
  9.2 0.3 pad_maximum_fusion
  9.6 36.1 %all_to_all.24 = bf16[4,256,1280]{2,1,0:T(8,128)(2,1)S(1)} all-to-all(bf16[4,256,1280]{2,1,0:T(8,128)(2,1)S(1)} %pad_maximum_fusion), channel_id=1, replica_groups=mesh['dp'=4,'vocab'=8] {'dp'}, dimensions={0} | all-to-all | bytes 5242880 | tf_op jit(solution)/shard_map/all_to_all | solution.py:10
  45.7 0.0 copy-start.2
  45.7 1.5 copy-done.2
  47.2 0.0 slice-done
  47.2 0.0 slice-done.1
  47.2 9.3 %fusion.7 = f32[1024,2432]{1,0:T(8,128)} fusion(bf16[1024,1280]{1,0:T(8,128)(2,1)S(1)} %bitcast.25, bf16[1280,2432]{1,0:T(8,128)(2,1)S(1)} %bitcast.31), kind=kOutput, calls=%fused_computation.15 | convolution fusion | flops 6375342080 | bytes 18808832 | tf_op jit(solution)/shard_map/dot_general | solution.py:28
  56.5 0.0 reduce-scatter.3.cloned.1.call-update
  56.5 0.0 copy-start.4
  56.5 0.0 all-gather.3.cloned.1.call-start
  56.6 99.0 %reduce-scatter.3.cloned.1.call-done = f32[256,2432]{1,0:T(8,128)} async-done(((f32[1024,2432]{1,0:T(8,128)}), f32[256,2432]{1,0:T(8,128)}) %reduce-scatter.3.cloned.1.call-update) | async-done | bytes 2490384 | tf_op jit(solution)/shard_map/reduce_scatter | solution.py:27
  155.6 0.0 copy-start
  155.6 2.1 reduce_max.9
  157.6 16.2 %pmax.7 = f32[256]{0:T(256)S(1)} all-reduce(f32[256]{0:T(256)S(1)} %reduce_max.9), channel_id=1, replica_groups=mesh['dp'=4,'vocab'=8] {'vocab'}, use_global_device_ids=true, to_apply=%region_2.0 | all-reduce | flops 256 | bytes 2048 | tf_op jit(solution)/shard_map/pmax | solution.py:33
  173.8 0.0 copy-done
  173.8 0.5 fusion.6
  174.3 13.6 %psum.7 = f32[256]{0:T(256)S(1)} all-reduce(f32[256]{0:T(256)S(1)} %fusion.6), channel_id=1, replica_groups=mesh['dp'=4,'vocab'=8] {'vocab'}, use_global_device_ids=true, to_apply=%region_4.0 | all-reduce | flops 256 | bytes 2048 | tf_op jit(solution)/shard_map/psum | solution.py:35
  187.9 0.0 copy-done.4
  187.9 1.8 subtract_convert_fusion
  189.7 0.0 all-gather.3.cloned.1.call-update
  189.7 0.0 reduce-scatter.5.cloned.1.call-start
  189.7 56.5 %all-gather.3.cloned.1.call-done = bf16[1024,2432]{1,0:T(8,128)(2,1)} async-done(((bf16[256,2432]{1,0:T(8,128)(2,1)}), bf16[1024,2432]{1,0:T(8,128)(2,1)}) %all-gather.3.cloned.1.call-update) | async-done | bytes 4980752 | tf_op jit(solution)/shard_map/all_gather | solution.py:38
  246.2 12.2 %fusion.8 = f32[1024,1280]{1,0:T(8,128)} fusion(bf16[1024,2432]{1,0:T(8,128)(2,1)} %all-gather.3.cloned.1.call-done, bf16[1280,2432]{1,0:T(8,128)(2,1)} %param.6), kind=kOutput, calls=%fused_computation.16 | convolution fusion | flops 6375342080 | bytes 16449536 | tf_op jit(solution)/shard_map/dot_general | solution.py:43
  258.4 0.0 copy-start.1
  258.4 0.0 reduce-scatter.5.cloned.1.call-update
  258.4 1.7 copy-done.1
  260.1 2.5 copy.13
  262.7 0.0 copy-start.5
  262.7 3.8 %all-to-all-start.1 = ((bf16[256,4,1280]{0,2,1:T(8,128)(2,1)}), bf16[256,4,1280]{0,2,1:T(8,128)(2,1)S(1)}, u32[]{:S(2)}, u32[]{:S(2)}) async-start(bf16[256,4,1280]{0,2,1:T(8,128)(2,1)} %bitcast.24), calls=%async_computation.2 | async-start | bytes 5242880 | tf_op jit(solution)/shard_map/all_to_all | solution.py:21
  266.5 0.0 copy-done.5
  266.5 32.2 %all-gather = s32[4,1,256]{2,1,0:T(1,128)S(1)} all-gather(s32[1,1,256]{2,1,0:T(1,128)S(1)} %bitcast.29), channel_id=1, replica_groups=mesh['dp'=4,'vocab'=8] {'dp'}, dimensions={0}, use_global_device_ids=true | all-gather | bytes 5120 | tf_op jit(solution)/shard_map/all_gather | solution.py:17
  298.7 0.0 all-to-all-done.1
  298.7 2.6 copy.14
  301.2 10.9 %fusion.1 = bf16[1280,2432]{0,1:T(8,128)(2,1)} fusion(bf16[1024,1280]{1,0:T(8,128)(2,1)} %bitcast.27, s32[2432]{0:T(1024)S(1)} %iota_add_fusion, s32[1024]{0:T(1024)S(1)} %bitcast.28), kind=kOutput, calls=%fused_computation.3 | convolution fusion | flops 6380945408 | bytes 8861184 | tf_op jit(solution)/shard_map/dot_general | solution.py:24
  312.1 0.0 copy-start.3
  312.1 9.5 %copy.15 = bf16[1280,2432]{1,0:T(8,128)(2,1)} copy(bf16[1280,2432]{0,1:T(8,128)(2,1)} %fusion.1) | data formatting | bytes 12451840
  321.6 0.0 copy-done.3
  321.6 11.3 %convolution_convert_fusion.1 = bf16[1280,2432]{1,0:T(8,128)(2,1)} fusion(bf16[1024,1280]{1,0:T(8,128)(2,1)S(1)} %bitcast.26, bf16[1024,2432]{1,0:T(8,128)(2,1)} %all-gather.3.cloned.1.call-done), kind=kOutput, calls=%fused_computation.1 | convolution fusion | flops 6378455040 | bytes 13828096 | tf_op jit(solution)/shard_map/dot_general | solution.py:39
  332.9 0.0 reduce-scatter.5.cloned.1.call-done
  332.9 1.8 convert_element_type.24
  (2 shorter events, 0.0 us)
Async XLA Ops:
  7.2 148.4 %reduce-scatter.3.cloned.1.call-start = ((), (), s32[]{:S(2)}) async-start(), calls=%async_computation.4 | async-start | bytes 12451840 | tf_op jit(solution)/shard_map/reduce_scatter | solution.py:27
  7.2 40.0 %slice-start = ((s8[6225920]{0:T(1024)(128)(4,1)}), s8[4194304]{0:T(1024)(128)(4,1)S(1)}, s32[]{:S(2)}) async-start(s8[6225920]{0:T(1024)(128)(4,1)} %bitcast.30), calls=%async_computation.7 | async-start | bytes 8388608
  9.2 38.0 %slice-start.1 = ((s8[6225920]{0:T(1024)(128)(4,1)}), s8[2031616]{0:T(1024)(128)(4,1)S(1)}, s32[]{:S(2)}) async-start(s8[6225920]{0:T(1024)(128)(4,1)} %bitcast.30), calls=%async_computation.8 | async-start | bytes 4063232
  45.7 1.5 copy-start.2
  56.5 131.4 %copy-start.4 = (s32[256]{0:T(256)S(1)}, s32[256]{0:T(256)}, u32[]{:S(2)}) copy-start(s32[256]{0:T(256)} %param.7) | copy-start | bytes 3076
  56.5 189.6 %all-gather.3.cloned.1.call-start = ((), (), s32[]{:S(2)}) async-start(), calls=%async_computation.5 | async-start | bytes 6225920 | tf_op jit(solution)/shard_map/all_gather | solution.py:38
  155.6 18.3 %copy-start = (f32[256,2432]{1,0:T(8,128)S(1)}, f32[256,2432]{1,0:T(8,128)}, u32[]{:S(2)}) copy-start(f32[256,2432]{1,0:T(8,128)} %reduce-scatter.3.cloned.1.call-done) | copy-start | bytes 7471108
  189.7 143.2 %reduce-scatter.5.cloned.1.call-start = ((), (), s32[]{:S(2)}) async-start(), calls=%async_computation.6 | async-start | bytes 5898240 | tf_op jit(solution)/shard_map/reduce_scatter | solution.py:42
  258.4 1.7 copy-start.1
  262.7 3.8 %copy-start.5 = (s32[256]{0:T(256)S(1)}, s32[256]{0:T(256)}, u32[]{:S(2)}) copy-start(s32[256]{0:T(256)} %param.8) | copy-start | bytes 3076
  262.7 36.0 %all-to-all-start.1 = ((bf16[256,4,1280]{0,2,1:T(8,128)(2,1)}), bf16[256,4,1280]{0,2,1:T(8,128)(2,1)S(1)}, u32[]{:S(2)}, u32[]{:S(2)}) async-start(bf16[256,4,1280]{0,2,1:T(8,128)(2,1)} %bitcast.24), calls=%async_computation.2 | async-start | bytes 5242880 | tf_op jit(solution)/shard_map/all_to_all | solution.py:21
  312.1 9.5 %copy-start.3 = (bf16[4,256,1280]{2,1,0:T(8,128)(2,1)S(1)}, bf16[4,256,1280]{2,1,0:T(8,128)(2,1)}, u32[]{:S(2)}) copy-start(bf16[4,256,1280]{2,1,0:T(8,128)(2,1)} %copy-done.2) | copy-start | bytes 7864324
Sparse Core Ops, SparseCore 0:
  56.7 98.8 reduce-scatter.2
  189.8 56.3 all-gather.2
  258.5 59.8 reduce-scatter.4
